TPU v7x, 32 devices: a whole 2x2x4 slice. The times are simulated.
32 devices in a mesh: row: 8 (over y, x, core), col: 4 (over z).
Axes of the slice: x: 2, y: 2, z: 4, core: 2. Of those that a mesh axis runs over, the one named last changes fastest.
Arguments:
- chol: bfloat16 [3, 6144, 2048], P(None, 'row', 'col'), may hold values from -0.67578125 to 0.67578125
- amps: bfloat16 [9, 2048, 2048], P(None, 'row', 'col'), may hold values from -0.19921875 to 0.19921875
- eps_occ: float32 [3], replicated, may hold values from -2 to -0.5
- eps_vir: float32 [2048], replicated, may hold values from 1 to 8
- pairs: int32 [9, 2], replicated, may hold values from 0 to 2, as said below
Outputs:
- residual: float32 [9, 2048, 2048], P(None, 'row', 'col')
Inputs may be any that keep to these rules, and one draw needn't show every extreme that they name: `pairs`: the rows list every ordered pair (i, j) of orbitals 0 to 2 exactly once.
All inputs are finite; a program needn't handle non-finite values.
Results may differ from a plain program's by a relative error of at most 0.0039.
Values may be sent and summed in bfloat16 or wider, within the bound.
A program may use at most 128 MiB of HBM per device.

v0:
```python
import jax
import jax.numpy as jnp
from jax import lax
from jax.sharding import PartitionSpec as P


def from_root(block, axis, source):
    block = jnp.where(lax.axis_index(axis) == source, block, jnp.zeros_like(block))
    return lax.psum(block, axis)


def per_device(chol, amps, eps_occ, eps_vir, pairs):
    row_index = lax.axis_index("row")
    col_index = lax.axis_index("col")
    occ = chol.shape[0]
    slabs = amps.shape[0]
    tile_rows = amps.shape[1]
    tile_cols = amps.shape[2]
    offset = row_index % 2 * tile_rows
    flat_pair = pairs[:, 0] * occ + pairs[:, 1]
    matches = (flat_pair[None, :] == jnp.arange(slabs, dtype=jnp.int32)[:, None]).astype(jnp.int32)
    slot = jnp.sum(matches * jnp.arange(slabs, dtype=jnp.int32)[None, :], axis=1)
    grid = jnp.take(amps, slot, axis=0).reshape(occ, occ, tile_rows, tile_cols)
    col_panels = lax.all_gather(chol, "row", axis=1, tiled=True)
    own_rows = lax.dynamic_slice_in_dim(col_panels, offset, tile_rows, 2)
    row_panels = from_root(own_rows, "col", row_index // 2)
    coulomb = lax.dot_general(
        row_panels, col_panels, (((1,), (1,)), ((), ())), preferred_element_type=jnp.float32
    )
    coulomb_b = coulomb.astype(jnp.bfloat16)
    left_rows = lax.all_gather(coulomb_b, "col", axis=3, tiled=True)
    left = left_rows
    dressing = lax.dot_general(
        left,
        lax.all_gather(grid, "row", axis=2, tiled=True),
        (((2, 3), (0, 2)), ((), ())),
        preferred_element_type=jnp.float32,
    )
    dressed = coulomb + dressing
    dressed_b = dressed.astype(jnp.bfloat16)
    amp_rows = lax.all_gather(grid, "col", axis=3, tiled=True)
    left = amp_rows
    quadratic = lax.dot_general(
        left,
        lax.all_gather(dressed_b, "row", axis=1, tiled=True),
        (((1, 3), (0, 1)), ((), ())),
        preferred_element_type=jnp.float32,
    )
    eps_rows = lax.dynamic_slice_in_dim(eps_vir, row_index * tile_rows, tile_rows, 0)
    eps_cols = lax.dynamic_slice_in_dim(eps_vir, col_index * tile_cols, tile_cols, 0)
    denom = (
        eps_rows[None, :, None, None]
        + eps_cols[None, None, None, :]
        - eps_occ[:, None, None, None]
        - eps_occ[None, None, :, None]
    )
    amp_float = jnp.transpose(grid, (0, 2, 1, 3)).astype(jnp.float32)
    result = denom * amp_float + dressed + quadratic
    ordered = jnp.transpose(result, (0, 2, 1, 3)).reshape(occ * occ, tile_rows, tile_cols)
    return jnp.take(ordered, flat_pair, axis=0)


def solution(mesh):
    placed = (P(None, "row", "col"), P(None, "row", "col"), P(), P(), P())
    return jax.shard_map(
        per_device, mesh=mesh, in_specs=placed, out_specs=P(None, "row", "col"), check_vma=False
    )
```

profile of v0, /device:TPU:0, one launch (start us, length us, event | category | flops | bytes accessed | tf_op | source)
XLA Modules:
  0.0 1017.2 jit_solution(9229886071944885983)
XLA Ops:
  6.5 0.0 copy-start
  6.5 0.0 all-gather.6.cloned.1.call-start
  6.5 0.7 all-gather.6.cloned.1.call-update
  7.3 0.0 all-reduce.2.cloned.1.call-start
  7.3 103.3 %all-gather.6.cloned.1.call-done = bf16[3,6144,512]{2,1,0:T(8,128)(2,1)} async-done(((bf16[3,768,512]{2,1,0:T(8,128)(2,1)}), bf16[3,6144,512]{2,1,0:T(8,128)(2,1)}) %all-gather.6.cloned.1.call-update) | async-done | bytes 18874384 | tf_op jit(solution)/shard_map/all_gather | solution.py:24
  110.6 8.8 dynamic-slice_select_fusion
  119.4 0.0 copy-start.3
  119.4 0.0 all-reduce.2.cloned.1.call-update
  119.5 0.0 all-gather.10.cloned.1.call-start
  119.5 0.6 copy-done.3
  120.1 0.1 select_reduce_fusion
  120.2 0.1 reduce_sum.14
  120.3 0.0 copy-done
  120.3 2.3 gather_fusion
  122.6 3.4 broadcast_select_fusion.1
  126.1 0.0 all-gather.10.cloned.1.call-update
  126.1 0.0 all-gather.8.cloned.1.call-start
  126.1 318.1 %all-reduce.2.cloned.1.call-done = bf16[3,6144,256]{2,1,0:T(8,128)(2,1)} async-done(((bf16[3,6144,256]{2,1,0:T(8,128)(2,1)}), bf16[3,6144,256]{2,1,0:T(8,128)(2,1)}) %all-reduce.2.cloned.1.call-update) | async-done | bytes 9437200 | tf_op jit(solution)/shard_map/psum | solution.py:9
  444.3 22.1 %fusion.21 = (bf16[3,256,3,512]{3,1,2,0:T(8,128)(2,1)}, f32[3,256,3,512]{3,1,2,0:T(8,128)}) fusion(bf16[3,6144,512]{2,1,0:T(8,128)(2,1)} %all-gather.6.cloned.1.call-done, bf16[3,6144,256]{2,1,0:T(8,128)(2,1)} %all-reduce.2.cloned.1.call-done), kind=kOutput, calls=%fused_computation.33 | convolution fusion | flops 14496694272 | bytes 35389440 | tf_op jit(solution)/shard_map/dot_general | solution.py:27
  466.4 0.0 all-gather.8.cloned.1.call-update
  466.4 0.0 all-gather.12.cloned.1.call-start
  466.4 0.5 all-gather.12.cloned.1.call-update
  467.0 0.2 all-gather.14.cloned.1.call-start
  467.2 76.6 %all-gather.10.cloned.1.call-done = bf16[3,3,2048,512]{3,2,1,0:T(8,128)(2,1)} async-done(((bf16[3,3,256,512]{3,2,1,0:T(8,128)(2,1)}), bf16[3,3,2048,512]{3,2,1,0:T(8,128)(2,1)}) %all-gather.10.cloned.1.call-update) | async-done | bytes 18874384 | tf_op jit(solution)/shard_map/all_gather | solution.py:35
  543.8 168.2 %all-gather.8.cloned.1.call-done = bf16[3,256,3,2048]{3,1,2,0:T(8,128)(2,1)} async-done(((bf16[3,256,3,512]{3,1,2,0:T(8,128)(2,1)}), bf16[3,256,3,2048]{3,1,2,0:T(8,128)(2,1)}) %all-gather.8.cloned.1.call-update) | async-done | bytes 9437200 | tf_op jit(solution)/shard_map/all_gather | solution.py:31
  712.0 0.0 copy-start.4
  712.0 22.5 %fusion.22 = (bf16[3,256,3,512]{3,1,2,0:T(8,128)(2,1)}, f32[3,256,3,512]{3,1,2,0:T(8,128)}) fusion(f32[3,256,3,512]{3,1,2,0:T(8,128)} %get-tuple-element.8, bf16[3,3,2048,512]{3,2,1,0:T(8,128)(2,1)} %all-gather.10.cloned.1.call-done, bf16[3,256,3,2048]{3,1,2,0:T(8,128)(2,1)} %all-gather.8.cloned.1.call-done), kind=kOutput, calls=%fused_computation.34 | convolution fusion | flops 14497873920 | bytes 40108032 | tf_op jit(solution)/shard_map/dot_general | solution.py:33
  734.5 0.0 copy-start.2
  734.5 0.0 all-gather.14.cloned.1.call-update
  734.5 0.9 dynamic_slice.9
  735.4 0.8 dynamic_slice.10
  736.2 0.1 broadcast_add_fusion
  736.3 0.0 copy-done.4
  736.3 1.5 broadcast_subtract_fusion
  737.8 140.5 %all-gather.12.cloned.1.call-done = bf16[3,3,256,2048]{3,2,1,0:T(8,128)(2,1)} async-done(((bf16[3,3,256,512]{3,2,1,0:T(8,128)(2,1)}), bf16[3,3,256,2048]{3,2,1,0:T(8,128)(2,1)}) %all-gather.12.cloned.1.call-update) | async-done | bytes 9437200 | tf_op jit(solution)/shard_map/all_gather | solution.py:41
  878.4 98.6 %all-gather.14.cloned.1.call-done = bf16[3,2048,3,512]{3,1,2,0:T(8,128)(2,1)} async-done(((bf16[3,256,3,512]{3,1,2,0:T(8,128)(2,1)}), bf16[3,2048,3,512]{3,1,2,0:T(8,128)(2,1)}) %all-gather.14.cloned.1.call-update) | async-done | bytes 18874384 | tf_op jit(solution)/shard_map/all_gather | solution.py:45
  976.9 0.0 copy-done.2
  976.9 22.7 %bitcast_add_fusion = f32[3,3,256,512]{3,2,1,0:T(8,128)} fusion(f32[3,256,3,512]{3,1,2,0:T(8,128)} %get-tuple-element.10, bf16[3,3,256,512]{3,2,1,0:T(8,128)(2,1)S(1)} %copy-done.2, f32[3]{0:T(128)S(1)} %copy-done.4, f32[3,256,512]{2,1,0:T(8,128)} %broadcast_subtract_fusion, bf16[3,2048,3,512]{3,1,2,0:T(8,128)(2,1)} %all-gather.14.cloned.1.call-done, ...), kind=kOutput, calls=%fused_computation.14 | convolution fusion | flops 14501412864 | bytes 41680908 | tf_op jit(solution)/shard_map/dot_general | solution.py:43
  999.6 5.3 gather_fusion.1
  1004.9 0.0 copy-start.1
  1004.9 5.4 broadcast_select_fusion
  1010.4 0.0 copy-done.1
  (6 shorter events, 0.0 us)
Async XLA Ops:
  6.5 113.8 %copy-start = (bf16[9,256,512]{2,1,0:T(8,128)(2,1)S(1)}, bf16[9,256,512]{2,1,0:T(8,128)(2,1)}, u32[]{:S(2)}) copy-start(bf16[9,256,512]{2,1,0:T(8,128)(2,1)} %param.6) | copy-start | bytes 7077892
  6.5 104.1 %all-gather.6.cloned.1.call-start = ((), (), s32[]{:S(2)}) async-start(), calls=%async_computation | async-start | bytes 21233664 | tf_op jit(solution)/shard_map/all_gather | solution.py:24
  7.3 437.0 %all-reduce.2.cloned.1.call-start = ((), (), s32[]{:S(2)}) async-start(), calls=%async_computation.1 | async-start | bytes 18874368 | tf_op jit(solution)/shard_map/psum | solution.py:9
  119.4 0.7 copy-start.3
  119.5 424.3 %all-gather.10.cloned.1.call-start = ((), (), s32[]{:S(2)}) async-start(), calls=%async_computation.3 | async-start | bytes 21233664 | tf_op jit(solution)/shard_map/all_gather | solution.py:35
  126.1 585.9 %all-gather.8.cloned.1.call-start = ((), (), s32[]{:S(2)}) async-start(), calls=%async_computation.2 | async-start | bytes 11796480 | tf_op jit(solution)/shard_map/all_gather | solution.py:31
  466.4 412.0 %all-gather.12.cloned.1.call-start = ((), (), s32[]{:S(2)}) async-start(), calls=%async_computation.4 | async-start | bytes 11796480 | tf_op jit(solution)/shard_map/all_gather | solution.py:41
  467.0 510.0 %all-gather.14.cloned.1.call-start = ((), (), s32[]{:S(2)}) async-start(), calls=%async_computation.5 | async-start | bytes 21233664 | tf_op jit(solution)/shard_map/all_gather | solution.py:45
  712.0 24.3 %copy-start.4 = (f32[3]{0:T(128)S(1)}, f32[3]{0:T(128)}, u32[]{:S(2)}) copy-start(f32[3]{0:T(128)} %param.7) | copy-start | bytes 40
  734.5 242.4 %copy-start.2 = (bf16[3,3,256,512]{3,2,1,0:T(8,128)(2,1)S(1)}, bf16[3,3,256,512]{3,2,1,0:T(8,128)(2,1)}, u32[]{:S(2)}) copy-start(bf16[3,3,256,512]{3,2,1,0:T(8,128)(2,1)} %broadcast_select_fusion.1) | copy-start | bytes 7077892
  1004.9 5.4 copy-start.1
Sparse Core Ops, SparseCore 0:
  9.2 101.3 all-gather.5
  119.6 324.6 all-reduce.1
  446.2 97.5 all-gather.9
  545.2 166.7 all-gather.7
  713.4 164.9 all-gather.11
  880.1 96.7 all-gather.13
where the time goes:
time: 1020 us
  waiting for transfers between devices  907 us (89%)
  matrix products  67.3 us (7%)
  other arithmetic  19.5 us (2%)
  between operations  13.5 us (1%)
    psum x1, waiting for transfers between devices, from_root(): return lax.psum(block, axis)  318 us
    all_gather x1, waiting for transfers between devices, per_device(): left_rows = lax.all_gather(coulomb_b, 'col', axis=3, tiled=True)  168 us
    all_gather x1, waiting for transfers between devices, per_device(): amp_rows = lax.all_gather(grid, 'col', axis=3, tiled=True)  141 us
    all_gather x1, waiting for transfers between devices, per_device(): col_panels = lax.all_gather(chol, 'row', axis=1, tiled=True)  103 us
    all_gather x1, waiting for transfers between devices, per_device(): lax.all_gather(dressed_b, 'row', axis=1, tiled=True)  98.6 us
    all_gather x1, waiting for transfers between devices, per_device(): lax.all_gather(grid, 'row', axis=2, tiled=True)  76.6 us
    dot_general x1, matrix products, per_device(): lax.dot_general(left, lax.all_gather(dressed_b, 'row', axis=1, tiled=True...  22.7 us
    dot_general x1, matrix products, per_device(): lax.dot_general(left, lax.all_gather(grid, 'row', axis=2, tiled=True), ((...  22.5 us
  transfers between devices with their start and end apart: 6, of which 6 were waited for; matrix products, arithmetic and copies ran while one was open for 5% of the time, Pallas kernels for 0%

commit v1 on v0

v1 whole, which is shorter than its diff:
```python
import functools

import jax
import jax.numpy as jnp
from jax import lax
from jax.experimental import pallas as pl
from jax.experimental.pallas import tpu as pltpu
from jax.sharding import PartitionSpec as P

F32 = jnp.float32
BF16 = jnp.bfloat16
MESH = pl.DeviceIdType.MESH
SPLIT_ROWS = 8


def remote(src, dst, send, recv, index, row):
    return pltpu.make_async_remote_copy(
        src_ref=src,
        dst_ref=dst,
        send_sem=send.at[index],
        recv_sem=recv.at[index],
        device_id={"row": row},
        device_id_type=MESH,
    )


def gather_kernel(size, x_ref, out_ref, own, local, send, recv):
    me = lax.axis_index("row")
    core = lax.rem(me, 2)
    xbit = lax.rem(me // 2, 2)
    ybit = me // 4
    sib = me + 1 - 2 * core
    xn = me + 2 - 4 * xbit
    yn = me + 4 - 8 * ybit
    far = xn + 4 - 8 * ybit
    half = size // 2

    def part(origin, low, count):
        return out_ref.at[:, pl.ds(pl.multiple_of(origin * size + low, 16), count), :]

    c0 = remote(x_ref, part(me, 0, size), send, recv, 0, xn)
    c1 = remote(x_ref, part(me, 0, size), send, recv, 1, yn)
    c2 = remote(x_ref, part(me, 0, size), send, recv, 2, sib)
    c0.start()
    c1.start()
    c2.start()
    bring = pltpu.make_async_copy(x_ref, own, local.at[0])
    bring.start()
    bring.wait()
    place = pltpu.make_async_copy(own, part(me, 0, size), local.at[1])
    place.start()
    c0.wait_recv()
    c3 = remote(part(xn, 0, half), part(xn, 0, half), send, recv, 3, yn)
    c4 = remote(part(xn, 0, size), part(xn, 0, size), send, recv, 4, sib)
    c3.start()
    c4.start()
    c1.wait_recv()
    c5 = remote(part(yn, half, half), part(yn, half, half), send, recv, 5, xn)
    c6 = remote(part(yn, 0, size), part(yn, 0, size), send, recv, 6, sib)
    c5.start()
    c6.start()
    c3.wait_recv()
    c7 = remote(part(far, 0, half), part(far, 0, half), send, recv, 7, sib)
    c7.start()
    c5.wait_recv()
    c8 = remote(part(far, half, half), part(far, half, half), send, recv, 8, sib)
    c8.start()
    for copy in (c2, c4, c6, c7, c8):
        copy.wait_recv()
    for copy in (c0, c1, c2, c3, c4, c5, c6, c7, c8):
        copy.wait_send()
    place.wait()


def gather_rows(x):
    rows = lax.axis_size("row")
    if rows != SPLIT_ROWS:
        return lax.all_gather(x, "row", axis=1, tiled=True)
    lead, size, width = x.shape
    return pl.pallas_call(
        functools.partial(gather_kernel, size),
        out_shape=jax.ShapeDtypeStruct((lead, rows * size, width), x.dtype),
        in_specs=[pl.BlockSpec(memory_space=pl.ANY)],
        out_specs=pl.BlockSpec(memory_space=pl.ANY),
        scratch_shapes=[
            pltpu.VMEM(x.shape, x.dtype),
            pltpu.SemaphoreType.DMA((2,)),
            pltpu.SemaphoreType.DMA((9,)),
            pltpu.SemaphoreType.DMA((9,)),
        ],
        compiler_params=pltpu.CompilerParams(has_side_effects=True),
        cost_estimate=pl.CostEstimate(flops=0, bytes_accessed=16 * rows * x.size, transcendentals=0),
        name="gather_rows",
    )(x)


def swap_kernel(rows, x_ref, out_ref, own, local, send, recv):
    me = lax.axis_index("row")
    size = x_ref.shape[1]
    width = x_ref.shape[2] // rows

    def piece(dest):
        return x_ref.at[:, :, pl.ds(pl.multiple_of(dest * width, width), width)]

    def place(origin):
        return out_ref.at[:, pl.ds(pl.multiple_of(origin * size, size), size), :]

    copies = []
    for step in range(1, rows):
        dest = lax.rem(me + step, rows)
        copies.append(remote(piece(dest), place(me), send, recv, step, dest))
    for copy in copies:
        copy.start()
    bring = pltpu.make_async_copy(piece(me), own, local.at[0])
    bring.start()
    bring.wait()
    keep = pltpu.make_async_copy(own, place(me), local.at[1])
    keep.start()
    for copy in copies:
        copy.wait_recv()
    for copy in copies:
        copy.wait_send()
    keep.wait()


def swap_rows(x):
    rows = lax.axis_size("row")
    if rows != SPLIT_ROWS:
        return lax.all_to_all(x, "row", split_axis=2, concat_axis=1, tiled=True)
    lead, size, width = x.shape
    return pl.pallas_call(
        functools.partial(swap_kernel, rows),
        out_shape=jax.ShapeDtypeStruct((lead, rows * size, width // rows), x.dtype),
        in_specs=[pl.BlockSpec(memory_space=pl.ANY)],
        out_specs=pl.BlockSpec(memory_space=pl.ANY),
        scratch_shapes=[
            pltpu.VMEM((lead, size, width // rows), x.dtype),
            pltpu.SemaphoreType.DMA((2,)),
            pltpu.SemaphoreType.DMA((rows,)),
            pltpu.SemaphoreType.DMA((rows,)),
        ],
        compiler_params=pltpu.CompilerParams(has_side_effects=True),
        cost_estimate=pl.CostEstimate(flops=0, bytes_accessed=32 * x.size, transcendentals=0),
        name="swap_rows",
    )(x)


def per_device(chol, amps, eps_occ, eps_vir, pairs):
    row_index = lax.axis_index("row")
    col_index = lax.axis_index("col")
    occ, depth, _ = chol.shape
    slabs, tile_rows, tile_cols = amps.shape
    flat_pair = pairs[:, 0] * occ + pairs[:, 1]
    matches = (flat_pair[None, :] == jnp.arange(slabs, dtype=jnp.int32)[:, None]).astype(jnp.int32)
    slot = jnp.sum(matches * jnp.arange(slabs, dtype=jnp.int32)[None, :], axis=1)
    grid = jnp.take(amps, slot, axis=0, mode="clip").reshape(occ, occ, tile_rows, tile_cols)
    wide = jnp.transpose(grid, (0, 2, 1, 3)).reshape(occ, tile_rows, occ * tile_cols)

    half = depth // 2
    first, second = chol[:, :half], chol[:, half:]
    amp_cols = gather_rows(wide)
    rows_of_first = lax.all_gather(first, "col", axis=2, tiled=True)
    later, _ = lax.optimization_barrier((second, amp_cols))
    rows_of_second = lax.all_gather(later, "col", axis=2, tiled=True)

    def dress(part, chol_rows):
        y = lax.dot_general(
            chol_rows, amp_cols, (((0, 2), (0, 1)), ((), ())), preferred_element_type=F32
        )
        own = jnp.transpose(part, (1, 0, 2)).reshape(half, occ * tile_cols)
        y = (y + own.astype(F32)).astype(BF16)
        return swap_rows(chol_rows), gather_rows(y[None])[0]

    def close(chol_cols, y_cols):
        return lax.dot_general(
            chol_cols, y_cols, (((1,), (0,)), ((), ())), preferred_element_type=F32
        )

    cols_of_first, y_first = dress(first, rows_of_first)
    rows_of_second, held, cols_of_first, y_first, second = lax.optimization_barrier(
        (rows_of_second, grid, cols_of_first, y_first, second)
    )
    amp_rows = lax.all_gather(held, "col", axis=3, tiled=True)
    cols_of_second, y_second = dress(second, rows_of_second)
    dressed = close(cols_of_first, y_first) + close(cols_of_second, y_second)
    dressed_cols = gather_rows(dressed.astype(BF16))
    quadratic = lax.dot_general(
        amp_rows,
        dressed_cols.reshape(occ, -1, occ * tile_cols),
        (((1, 3), (0, 1)), ((), ())),
        preferred_element_type=F32,
    )
    eps_rows = lax.dynamic_slice_in_dim(eps_vir, row_index * tile_rows, tile_rows, 0)
    eps_cols = lax.dynamic_slice_in_dim(eps_vir, col_index * tile_cols, tile_cols, 0)
    denom = (
        eps_rows[None, :, None, None]
        + eps_cols[None, None, None, :]
        - eps_occ[:, None, None, None]
        - eps_occ[None, None, :, None]
    )
    amp_float = jnp.transpose(grid, (0, 2, 1, 3)).astype(F32)
    shape = (occ, tile_rows, occ, tile_cols)
    result = denom * amp_float + dressed.reshape(shape) + quadratic.reshape(shape)
    ordered = jnp.transpose(result, (0, 2, 1, 3)).reshape(occ * occ, tile_rows, tile_cols)
    return jnp.take(ordered, flat_pair, axis=0, mode="clip")


def solution(mesh):
    placed = (P(None, "row", "col"), P(None, "row", "col"), P(), P(), P())
    return jax.shard_map(
        per_device, mesh=mesh, in_specs=placed, out_specs=P(None, "row", "col"), check_vma=False
    )
```

time: 1020 us -> 541 us (0.53)
  waiting for transfers between devices: 907 us -> 0.09 us
  Pallas kernels: 0 us -> 398 us
  local copies, waits for them, and re-layouts: 9.96 us -> 41.2 us
    all_gather x5 -> x3, waiting for transfers between devices: 587 us -> 0.04 us  [the longest x1 0.02 us: per_device(): rows_of_first = lax.all_gather(first, 'col', axis=2, tiled=True)]
    pallas_call x0 -> x6, Pallas kernels: none -> 398 us  [the longest x4 285 us: gather_rows(): pl.pallas_call(functools.partial(gather_kernel, size), out_shape=jax.Shap...]
    psum x1 -> x0, waiting for transfers between devices: 318 us -> none  [from_root(): return lax.psum(block, axis)]
    select_n x5 -> x0, other arithmetic: 17.7 us -> none  [the longest x1 8.84 us: from_root(): jnp.where(lax.axis_index(axis) == source, block, jnp.zeros_like(block))]
    reshape x0 -> x3, local copies, waits for them, and re-layouts: none -> 14.8 us  [the longest x1 6.21 us: per_device(): quadratic.reshape(shape)]
    dot_general x3 -> x5, matrix products: 67.3 us -> 72.7 us  [the longest x2 28.1 us: dress(): lax.dot_general(chol_rows, amp_cols, (((0, 2), (0, 1)), ((), ())), prefer...]
  transfers between devices with their start and end apart: 6 -> 3, of which waited for: 6 -> 0; matrix products, arithmetic and copies ran while one was open for 5% -> 16% of each run, Pallas kernels for 0% -> 74%
where the time goes in v1:
time: 541 us
  Pallas kernels  398 us (74%)
  matrix products  72.7 us (13%)
  local copies, waits for them, and re-layouts  41.2 us (8%)
  other arithmetic  15.6 us (3%)
  between operations  13.3 us (2%)
    pallas_call x4, Pallas kernels, gather_rows(): pl.pallas_call(functools.partial(gather_kernel, size), out_shape=jax.Shap...  285 us
    pallas_call x2, Pallas kernels, swap_rows(): pl.pallas_call(functools.partial(swap_kernel, rows), out_shape=jax.ShapeD...  113 us
    dot_general x2, matrix products, dress(): lax.dot_general(chol_rows, amp_cols, (((0, 2), (0, 1)), ((), ())), prefer...  28.1 us
    dot_general x2, matrix products, close(): lax.dot_general(chol_cols, y_cols, (((1,), (0,)), ((), ())), preferred_el...  23.3 us
    dot_general x1, matrix products, per_device(): lax.dot_general(amp_rows, dressed_cols.reshape(occ, -1, occ * tile_cols),...  21.3 us
  transfers between devices with their start and end apart: 3, of which 0 were waited for; matrix products, arithmetic and copies ran while one was open for 16% of the time, Pallas kernels for 74%

profile of v1, /device:TPU:0, one launch (start us, length us, event | category | flops | bytes accessed | tf_op | source)
XLA Modules:
  0.0 540.8 jit_solution(17203268496539530298)
XLA Ops:
  6.5 0.0 copy-start
  6.5 0.0 copy-start.7
  6.5 0.0 all-gather.6.cloned.1.call-start
  6.5 4.3 convert_bitcast_fusion.1
  10.9 0.0 all-gather.6.cloned.1.call-update
  10.9 0.0 all-gather.4.cloned.1.call-start
  10.9 0.0 copy-done.7
  11.0 0.1 select_reduce_fusion
  11.1 0.0 copy-done
  11.1 2.3 gather_fusion
  13.4 2.8 copy.28
  16.2 2.5 copy.29.x_ref
  18.8 0.0 copy-start.4
  18.8 93.0 %gather_rows.4 = bf16[3,2048,1536]{2,1,0:T(8,128)(2,1)} custom-call(bf16[3,256,1536]{2,1,0:T(8,128)(2,1)} %copy.29.x_ref), custom_call_target="tpu_custom_call" | custom-call | bytes 150994944 | tf_op jit(solution)/shard_map/gather_rows/pallas_call | solution.py:80
  111.7 0.0 all-gather.4.cloned.1.call-update
  111.8 0.0 all-gather.8.cloned.1.call-start
  111.8 0.0 copy-done.4
  111.8 2.0 copy.32
  113.8 2.0 copy.33
  115.8 0.0 all-gather.6.cloned.1.call-done.x_ref
  115.8 14.6 %fusion.13.x_ref = bf16[1,384,1536]{2,1,0:T(8,128)(2,1)} fusion(f32[384,1536]{1,0:T(8,128)S(1)} %copy.33, bf16[3,384,2048]{2,1,0:T(8,128)(2,1)} %all-gather.6.cloned.1.call-done.x_ref, bf16[3,2048,1536]{2,1,0:T(8,128)(2,1)} %gather_rows.4), kind=kOutput, calls=%fused_computation.16 | convolution fusion | flops 7248936960 | bytes 27131904 | tf_op jit(solution)/shard_map/dot_general | solution.py:167
  130.4 49.7 %gather_rows.5 = bf16[1,3072,1536]{2,1,0:T(8,128)(2,1)} custom-call(bf16[1,384,1536]{2,1,0:T(8,128)(2,1)} %fusion.13.x_ref), custom_call_target="tpu_custom_call" | custom-call | bytes 75497472 | tf_op jit(solution)/shard_map/gather_rows/pallas_call | solution.py:80
  180.1 0.0 copy-start.6
  180.1 55.4 %swap_rows.2 = bf16[3,3072,256]{2,1,0:T(8,128)(2,1)} custom-call(bf16[3,384,2048]{2,1,0:T(8,128)(2,1)} %all-gather.6.cloned.1.call-done.x_ref), custom_call_target="tpu_custom_call" | custom-call | bytes 75497472 | tf_op jit(solution)/shard_map/swap_rows/pallas_call | solution.py:131
  235.6 0.0 copy-start.3
  235.6 0.0 all-gather.4.cloned.1.call-done.x_ref
  235.6 0.0 all-gather.8.cloned.1.call-update
  235.7 0.8 dynamic_slice.6
  236.5 0.8 dynamic_slice.7
  237.3 0.1 broadcast_add_fusion
  237.4 0.0 copy-done.6
  237.4 1.4 broadcast_subtract_fusion
  238.8 0.0 copy-done.3
  238.8 1.7 convert_bitcast_fusion
  240.6 2.0 copy.35
  242.6 2.0 copy.36
  244.5 0.0 copy-start.5
  244.5 57.8 %swap_rows.3 = bf16[3,3072,256]{2,1,0:T(8,128)(2,1)} custom-call(bf16[3,384,2048]{2,1,0:T(8,128)(2,1)} %all-gather.4.cloned.1.call-done.x_ref), custom_call_target="tpu_custom_call" | custom-call | bytes 75497472 | tf_op jit(solution)/shard_map/swap_rows/pallas_call | solution.py:131
  302.3 0.0 copy-done.5
  302.3 13.6 %fusion.14.x_ref = bf16[1,384,1536]{2,1,0:T(8,128)(2,1)} fusion(f32[384,1536]{1,0:T(8,128)S(1)} %copy-done.5, bf16[3,384,2048]{2,1,0:T(8,128)(2,1)} %all-gather.4.cloned.1.call-done.x_ref, bf16[3,2048,1536]{2,1,0:T(8,128)(2,1)} %gather_rows.4), kind=kOutput, calls=%fused_computation.17 | convolution fusion | flops 7248936960 | bytes 27131904 | tf_op jit(solution)/shard_map/dot_general | solution.py:167
  315.9 0.0 slice-start
  315.9 52.5 %gather_rows.6 = bf16[1,3072,1536]{2,1,0:T(8,128)(2,1)} custom-call(bf16[1,384,1536]{2,1,0:T(8,128)(2,1)} %fusion.14.x_ref), custom_call_target="tpu_custom_call" | custom-call | bytes 75497472 | tf_op jit(solution)/shard_map/gather_rows/pallas_call | solution.py:80
  368.4 0.0 slice-start.1
  368.4 0.0 slice-start.2
  368.4 12.0 %fusion.2 = f32[3,256,1536]{2,1,0:T(8,128)S(1)} fusion(bf16[3,3072,256]{2,1,0:T(8,128)(2,1)} %swap_rows.3, bf16[1,3072,1536]{2,1,0:T(8,128)(2,1)} %gather_rows.6), kind=kOutput, calls=%fused_computation.4 | convolution fusion | flops 7247757312 | bytes 18874368 | tf_op jit(solution)/shard_map/dot_general | solution.py:175
  380.4 0.0 slice-done
  380.4 0.0 slice-done.1
  380.5 0.0 slice-done.2
  380.5 11.3 %fusion.15 = (bf16[3,256,1536]{2,1,0:T(8,128)(2,1)}, f32[3,256,1536]{2,1,0:T(8,128)}) fusion(f32[3,256,1536]{2,1,0:T(8,128)S(1)} %fusion.2, bf16[3,3072,256]{2,1,0:T(8,128)(2,1)} %swap_rows.2, bf16[3072,1536]{1,0:T(8,128)(2,1)S(1)} %bitcast.70), kind=kOutput, calls=%fused_computation.27 | convolution fusion | flops 7250116608 | bytes 25952256 | tf_op jit(solution)/shard_map/dot_general | solution.py:175
  391.8 89.4 %gather_rows.7 = bf16[3,2048,1536]{2,1,0:T(8,128)(2,1)} custom-call(bf16[3,256,1536]{2,1,0:T(8,128)(2,1)} %get-tuple-element.20.x_ref), custom_call_target="tpu_custom_call" | custom-call | bytes 150994944 | tf_op jit(solution)/shard_map/gather_rows/pallas_call | solution.py:80
  481.2 6.1 %copy.38 = f32[3,256,1536]{1,2,0:T(8,128)} copy(f32[3,256,1536]{2,1,0:T(8,128)} %get-tuple-element.21) | data formatting | bytes 9437184 | tf_op jit(solution)/shard_map/add | solution.py:185
  487.3 6.0 %copy.39 = f32[3,256,3,512]{3,1,2,0:T(8,128)} copy(f32[3,256,3,512]{1,3,2,0:T(8,128)} %bitcast.66) | data formatting | bytes 9437184 | tf_op jit(solution)/shard_map/reshape | solution.py:203
  493.3 0.0 all-gather.8.cloned.1.call-done
  493.3 21.3 %fusion = f32[3,256,1536,1]{1,2,3,0:T(8,128)} fusion(bf16[3,3,256,2048]{3,2,1,0:T(8,128)(2,1)} %all-gather.8.cloned.1.call-done, bf16[3,2048,1536]{2,1,0:T(8,128)(2,1)} %gather_rows.7), kind=kOutput, calls=%fused_computation.2 | convolution fusion | flops 14495514624 | bytes 33030144 | tf_op jit(solution)/shard_map/dot_general | solution.py:187
  514.7 0.0 copy-start.2
  514.7 6.2 %copy.41 = f32[3,256,3,512]{3,1,2,0:T(8,128)} copy(f32[3,256,3,512]{1,3,2,0:T(8,128)} %bitcast.74) | data formatting | bytes 9437184 | tf_op jit(solution)/shard_map/reshape | solution.py:203
  520.9 0.0 copy-done.2
  520.9 7.9 %add_add_fusion = f32[3,256,3,512]{3,1,2,0:T(8,128)} fusion(f32[3,256,3,512]{3,1,2,0:T(8,128)} %copy.41, f32[3,256,3,512]{3,1,2,0:T(8,128)} %copy.39, bf16[3,256,3,512]{3,1,2,0:T(8,128)(2,1)S(1)} %bitcast.65, f32[3]{0:T(128)S(1)} %copy-done.6, f32[3,256,512]{2,1,0:T(8,128)} %broadcast_subtract_fusion), kind=kLoop, calls=%fused_computation.8 | loop fusion | flops 5898240 | bytes 18087948 | tf_op jit(solution)/shard_map/add | solution.py:203
  528.8 0.0 copy-start.1
  528.8 5.5 %gather_fusion.1 = f32[9,256,512]{2,1,0:T(8,128)} fusion(f32[9,256,512]{2,1,0:T(8,128)} %bitcast.67, s32[1024]{0:T(1024)S(1)} %pad_clamp_fusion), kind=kCustom, calls=%fused_computation.1 | custom fusion | bytes 9437220 | tf_op jit(solution)/shard_map/jit(_take)/gather | solution.py:205
  534.3 0.0 copy-done.1
  (4 shorter events, 0.0 us)
Async XLA Ops:
  6.5 4.5 copy-start
  6.5 4.4 copy-start.7
  6.5 109.3 %all-gather.6.cloned.1.call-start = ((), (), s32[]{:S(2)}) async-start(), calls=%async_computation.1 | async-start | bytes 5898240 | tf_op jit(solution)/shard_map/all_gather | solution.py:162
  10.9 224.7 %all-gather.4.cloned.1.call-start = ((), (), s32[]{:S(2)}) async-start(), calls=%async_computation | async-start | bytes 5898240 | tf_op jit(solution)/shard_map/all_gather | solution.py:164
  18.8 93.0 %copy-start.4 = (f32[384,3,512]{2,0,1:T(8,128)S(1)}, f32[384,3,512]{2,0,1:T(8,128)}, u32[]{:S(2)}) copy-start(f32[384,3,512]{2,0,1:T(8,128)} %get-tuple-element.17) | copy-start | bytes 7077892
  111.8 381.6 %all-gather.8.cloned.1.call-start = ((), (), s32[]{:S(2)}) async-start(), calls=%async_computation.2 | async-start | bytes 11796480 | tf_op jit(solution)/shard_map/all_gather | solution.py:183
  180.1 57.2 %copy-start.6 = (f32[3]{0:T(128)S(1)}, f32[3]{0:T(128)}, u32[]{:S(2)}) copy-start(f32[3]{0:T(128)} %param.7) | copy-start | bytes 40
  235.6 3.2 copy-start.3
  244.5 57.8 %copy-start.5 = (f32[384,1536]{1,0:T(8,128)S(1)}, f32[384,1536]{1,0:T(8,128)}, u32[]{:S(2)}) copy-start(f32[384,1536]{1,0:T(8,128)} %copy.36) | copy-start | bytes 7077892
  315.9 64.5 %slice-start = ((s8[9437184]{0:T(1024)(128)(4,1)}), s8[1048576]{0:T(1024)(128)(4,1)S(1)}, s32[]{:S(2)}) async-start(s8[9437184]{0:T(1024)(128)(4,1)} %bitcast.68), calls=%async_computation.3 | async-start | bytes 2097152
  368.4 12.0 %slice-start.1 = ((s8[9437184]{0:T(1024)(128)(4,1)}), s8[4194304]{0:T(1024)(128)(4,1)S(1)}, s32[]{:S(2)}) async-start(s8[9437184]{0:T(1024)(128)(4,1)} %bitcast.68), calls=%async_computation.4 | async-start | bytes 8388608
  368.4 12.0 %slice-start.2 = ((s8[9437184]{0:T(1024)(128)(4,1)}), s8[4194304]{0:T(1024)(128)(4,1)S(1)}, s32[]{:S(2)}) async-start(s8[9437184]{0:T(1024)(128)(4,1)} %bitcast.68), calls=%async_computation.5 | async-start | bytes 8388608
  514.7 6.2 %copy-start.2 = (bf16[9,256,512]{2,1,0:T(8,128)(2,1)S(1)}, bf16[9,256,512]{2,1,0:T(8,128)(2,1)}, u32[]{:S(2)}) copy-start(bf16[9,256,512]{2,1,0:T(8,128)(2,1)} %gather_fusion) | copy-start | bytes 7077892
  528.8 5.5 %copy-start.1 = (bf16[9,256,512]{2,1,0:T(8,128)(2,1)S(1)}, bf16[9,256,512]{2,1,0:T(8,128)(2,1)}, u32[]{:S(2)}) copy-start(bf16[9,256,512]{2,1,0:T(8,128)(2,1)} %param.6) | copy-start | bytes 7077892
Sparse Core Ops, SparseCore 0:
  11.0 92.0 all-gather.5
  111.9 88.5 all-gather.3
  235.8 168.3 all-gather.7
